TPU v7x, 32 devices: a whole 2x2x4 slice. The times are simulated.
32 devices in a mesh: grp: 2 (over x), seq: 8 (over z, y), col: 2 (over core).
Axes of the slice: x: 2, y: 2, z: 4, core: 2. Of those that a mesh axis runs over, the one named last changes fastest.
Arguments:
- signal: bfloat16 [8192, 1408], P(('grp', 'seq'), 'col'), parts along dimension 0, may hold values from -6 to 6
- conv_weight: bfloat16 [5, 1408, 1408], P(None, None, 'col'), may hold values from -0.15625 to 0.15625
- conv_gain: float32 [1408], replicated, may hold values from 0.1 to 1.9
- embed_weight: bfloat16 [1408, 1536], P('col', 'seq'), may hold values from -0.15625 to 0.15625
- attn_gain: float32 [1536], replicated, may hold values from 0.1 to 1.9
- query_weight: bfloat16 [1536, 1024], P('seq'), may hold values from -4 to 4
- keyvalue_weight: bfloat16 [1536, 320], P('seq'), may hold values from -4 to 4
- output_weight: bfloat16 [1536, 1536], P(None, 'seq'), may hold values from -0.15625 to 0.15625
- rowcol_weight: bfloat16 [1536, 256], replicated, may hold values from -0.15625 to 0.15625
- pair_weight: bfloat16 [128, 128], replicated, may hold values from -0.5 to 0.5
Outputs:
- tokens: bfloat16 [2048, 1536], P(('grp', 'seq', 'col')), parts along dimension 0
- pair_out: bfloat16 [128, 64, 128], P(('grp', 'seq'), 'col'), parts along dimension 0
There are 2 independent parts, one for each index of `grp`. A program takes and returns all parts, laid end to end along the dimension named above; an argument that names none is the same for every part. Nothing has to cross between parts.
All inputs are finite; a program needn't handle non-finite values.
Results may differ from a plain program's by a relative error of at most 0.015.
Values may be sent and summed in bfloat16 or wider, within the bound.
A program may use at most 128 MiB of HBM per device.

v0:
```python
import jax
import jax.numpy as jnp
from jax import lax
from jax.sharding import PartitionSpec as P

DK = 128
DV = 192
POOL = 4
PAIR_POOL = 16


def with_halo(array, sides, width):
    for axis, dim in sides:
        size, length = (lax.axis_size(axis), array.shape[dim])
        up = [(i, (i + 1) % size) for i in range(size - 1)]
        down = [(j, i) for i, j in up]
        last = lax.slice_in_dim(array, length - width, length, axis=dim)
        first = lax.slice_in_dim(array, 0, width, axis=dim)
        before = lax.ppermute(last, axis, up)
        after = lax.ppermute(first, axis, down)
        array = jnp.concatenate([before, array, after], axis=dim)
    return array


def rms_scale(values, gain_vector):
    return (
        values * lax.rsqrt(jnp.mean(values * values, axis=-1, keepdims=True) + 1e-06) * gain_vector
    )


def attention_parts(queries, head_count):
    query_rows = queries.reshape(queries.shape[0] * head_count, DK)

    def absorb(running, pieces, first_row):
        running_max, running_sum, accumulated = running
        key_piece, value_piece = pieces
        scores = lax.dot_general(
            query_rows, key_piece, (((1,), (1,)), ((), ())), preferred_element_type=jnp.float32
        )
        newest_max = jnp.maximum(running_max, jnp.max(scores, axis=1))
        weights = jnp.exp(scores - newest_max[:, None])
        running_sum = jnp.sum(weights, axis=1)
        accumulated = jnp.dot(
            weights.astype(jnp.bfloat16), value_piece, preferred_element_type=jnp.float32
        )
        return (newest_max, running_sum, accumulated)

    row_count = query_rows.shape[0]
    initial = (
        jnp.full((row_count,), -1e30, jnp.float32),
        jnp.zeros((row_count,), jnp.float32),
        jnp.zeros((row_count, DV), jnp.float32),
    )
    return (absorb, initial)


def finish_attention(result, token_count):
    running_max, running_sum, accumulated = result
    return (accumulated / running_sum[:, None]).astype(jnp.bfloat16).reshape(token_count, -1)


def on_device(
    signal,
    conv_weight,
    conv_gain,
    embed_weight,
    attn_gain,
    query_weight,
    keyvalue_weight,
    output_weight,
    rowcol_weight,
    pair_weight,
):
    positions = signal.shape[0]
    tap_count = conv_weight.shape[0]
    halo_width = tap_count // 2
    padded = with_halo(signal, (("seq", 0),), halo_width)
    widened = lax.all_gather(padded, "col", axis=1, tiled=True)
    activated = jax.nn.gelu(
        rms_scale(widened.astype(jnp.float32), conv_gain), approximate=True
    ).astype(jnp.bfloat16)
    summed = signal.astype(jnp.float32)
    for tap_index in range(tap_count):
        summed = summed + jnp.dot(
            activated[tap_index : tap_index + positions],
            conv_weight[tap_index],
            preferred_element_type=jnp.float32,
        )
    pooled = jnp.mean(summed.reshape(positions // POOL, POOL, -1), axis=1).astype(jnp.bfloat16)
    embed_full = lax.all_gather(embed_weight, "seq", axis=1, tiled=True)
    col_count = lax.axis_size("col")
    embedded = lax.psum_scatter(
        jnp.dot(pooled, embed_full, preferred_element_type=jnp.float32).astype(jnp.bfloat16),
        "col",
        scatter_dimension=0,
        tiled=True,
    )
    normed = rms_scale(embedded.astype(jnp.float32), attn_gain).astype(jnp.bfloat16)
    head_count = query_weight.shape[1] // DK
    scaling = DK ** (-0.5)
    col_index = lax.axis_index("col")
    local_heads = head_count // col_count
    group_tokens = lax.all_gather(normed, "col", axis=0, tiled=True)
    group_count = group_tokens.shape[0]
    query_half = lax.dynamic_slice_in_dim(
        query_weight, col_index * local_heads * DK, local_heads * DK, 1
    )
    query_sum = jnp.dot(
        group_tokens,
        lax.all_gather(query_half, "seq", axis=0, tiled=True),
        preferred_element_type=jnp.float32,
    )
    keyvalue_sum = jnp.dot(
        group_tokens,
        lax.all_gather(keyvalue_weight, "seq", axis=0, tiled=True),
        preferred_element_type=jnp.float32,
    )
    queries = (query_sum * scaling).astype(jnp.bfloat16)
    keyvalue = keyvalue_sum.astype(jnp.bfloat16)
    absorb, initial = attention_parts(queries, local_heads)
    result = absorb(
        initial,
        (
            lax.all_gather(keyvalue[:, :DK], "seq", axis=0, tiled=True),
            lax.all_gather(keyvalue[:, DK:], "seq", axis=0, tiled=True),
        ),
        jnp.int32(0),
    )
    attended = finish_attention(result, group_count)
    output_half = lax.dynamic_slice_in_dim(
        output_weight, col_index * local_heads * DV, local_heads * DV, 0
    )
    partial_out = jnp.dot(
        attended,
        lax.all_gather(output_half, "seq", axis=1, tiled=True),
        preferred_element_type=jnp.float32,
    )
    attention_out = lax.psum_scatter(
        partial_out.astype(jnp.bfloat16), "col", scatter_dimension=0, tiled=True
    ).astype(jnp.float32)
    tokens = (embedded.astype(jnp.float32) + attention_out).astype(jnp.bfloat16)
    pair_pool = jnp.mean(
        tokens.astype(jnp.float32).reshape(-1, PAIR_POOL, tokens.shape[1]), axis=1
    ).astype(jnp.bfloat16)
    projected = jnp.dot(pair_pool, rowcol_weight, preferred_element_type=jnp.float32).astype(
        jnp.bfloat16
    )
    features = pair_weight.shape[0]
    row_block = lax.all_gather(projected, "col", axis=0, tiled=True)
    column_all = lax.all_gather(row_block[:, features:], "seq", axis=0, tiled=True)
    row_part = row_block[:, :features]
    column_span = column_all.shape[0] // col_count
    column_part = lax.dynamic_slice_in_dim(
        column_all, lax.axis_index("col") * column_span, column_span, 0
    )
    hidden = jax.nn.gelu(
        row_part.astype(jnp.float32)[:, None, :] + column_part.astype(jnp.float32)[None, :, :],
        approximate=True,
    ).astype(jnp.bfloat16)
    pair_out = jnp.dot(
        hidden.reshape(-1, features), pair_weight, preferred_element_type=jnp.float32
    ).astype(jnp.bfloat16)
    return (tokens, pair_out.reshape(row_part.shape[0], column_span, features))


def solution(mesh):
    placed = (
        P(("grp", "seq"), "col"),
        P(None, None, "col"),
        P(),
        P("col", "seq"),
        P(),
        P("seq", None),
        P("seq", None),
        P(None, "seq"),
        P(),
        P(),
    )
    return jax.shard_map(
        on_device,
        mesh=mesh,
        in_specs=placed,
        out_specs=(P(("grp", "seq", "col"), None), P(("grp", "seq"), "col", None)),
        check_vma=False,
    )
```

profile of v0, /device:TPU:0, one launch (start us, length us, event | category | flops | bytes accessed | tf_op | source)
XLA Modules:
  0.0 256.0 jit_solution(12248278608278916954)
XLA Ops:
  7.2 1.4 copy.19
  8.7 4.9 %collective-permute-start = (bf16[2,704]{1,0:T(2,128)(2,1)S(1)}, bf16[2,704]{1,0:T(2,128)(2,1)S(1)}, u32[]{:S(2)}, u32[]{:S(2)}) collective-permute-start(bf16[2,704]{1,0:T(2,128)(2,1)S(1)} %get-tuple-element.4), channel_id=1, source_target_pairs={{0,2},{2,4},{4,6},{6,8},{8,10},{10,12},{12,14},{1,3},{3,5},{5,7},{... | collective-permute-start | bytes 8456 | tf_op jit(solution)/shard_map/ppermute | solution.py:19
  13.6 1.3 collective-permute-start.1
  14.9 4.2 %collective-permute-done.1 = bf16[2,704]{1,0:T(2,128)(2,1)S(1)} collective-permute-done((bf16[2,704]{1,0:T(2,128)(2,1)S(1)}, bf16[2,704]{1,0:T(2,128)(2,1)S(1)}, u32[]{:S(2)}, u32[]{:S(2)}) %collective-permute-start.1) | collective-permute-done | bytes 2848 | tf_op jit(solution)/shard_map/ppermute | solution.py:20
  19.1 1.1 maximum_bitcast_fusion
  21.0 10.3 %all-gather.13.cloned.1.call-done = bf16[2,704,516]{1,2,0:T(8,128)(2,1)} async-done(((bf16[1,704,516]{1,2,0:T(8,128)(2,1)}), bf16[2,704,516]{1,2,0:T(8,128)(2,1)}) %all-gather.13.cloned.1.call-update) | async-done | bytes 1453072 | tf_op jit(solution)/shard_map/all_gather | solution.py:78
  31.4 4.3 %copy.22 = f32[2,704,516]{1,0,2:T(2,128)} copy(bf16[2,704,516]{1,2,0:T(8,128)(2,1)} %all-gather.13.cloned.1.call-done) | data formatting | bytes 4359168 | tf_op jit(solution)/shard_map/convert_element_type | solution.py:80
  35.6 5.3 %reshape.62 = f32[1408,516]{0,1:T(8,128)} reshape(f32[2,704,516]{1,0,2:T(2,128)} %copy.22) | data formatting | bytes 5812224 | tf_op jit(solution)/shard_map/convert_element_type | solution.py:80
  41.0 2.4 multiply_reduce_fusion
  43.9 1.2 fusion.7
  45.1 3.0 %fusion.16 = f32[512,704]{0,1:T(8,128)S(1)} fusion(bf16[5,1408,704]{1,2,0:T(8,128)(2,1)} %param.11, bf16[516,1408]{1,0:T(8,128)(2,1)S(1)} %fusion.7), kind=kOutput, calls=%fused_computation.21 | convolution fusion | flops 1015021568 | bytes 4866048 | tf_op jit(solution)/shard_map/dot_general | solution.py:84
  48.1 1.4 copy-done.4
  49.6 1.3 fusion.12
  50.9 1.3 fusion.10
  52.2 1.3 fusion.8
  53.6 1.5 add_add_fusion
  55.1 1.6 copy.23
  56.7 1.8 reshape.50
  59.5 27.1 %all-gather.7.cloned.1.call-done = bf16[704,1536]{0,1:T(8,128)(2,1)} async-done(((bf16[704,192]{0,1:T(8,128)(2,1)}), bf16[704,1536]{0,1:T(8,128)(2,1)}) %all-gather.7.cloned.1.call-update) | async-done | bytes 2162704 | tf_op jit(solution)/shard_map/all_gather | solution.py:90
  86.6 3.3 %convolution_convert_fusion.1 = bf16[128,1536]{1,0:T(8,128)(2,1)} fusion(bf16[704,1536]{0,1:T(8,128)(2,1)} %all-gather.7.cloned.1.call-done, f32[128,704]{1,0:T(8,128)S(1)} %reduce_sum.46), kind=kOutput, calls=%fused_computation.11 | convolution fusion | flops 277200896 | bytes 2916352 | tf_op jit(solution)/shard_map/dot_general | solution.py:93
  91.6 34.7 %all_gather.34 = bf16[1536,320]{1,0:T(8,128)(2,1)S(1)} all-gather(bf16[192,320]{1,0:T(8,128)(2,1)S(1)} %copy-done.6), channel_id=1, replica_groups=mesh['grp'=2,'seq'=8,'col'=2] {'seq'}, dimensions={0}, use_global_device_ids=true | all-gather | bytes 1105920 | tf_op jit(solution)/shard_map/all_gather | solution.py:115
  126.3 1.1 fusion.39
  128.4 2.3 all_gather.32
  131.2 17.2 %all-gather.9.cloned.1.call-done = bf16[1536,512]{1,0:T(8,128)(2,1)} async-done(((bf16[192,512]{1,0:T(8,128)(2,1)}), bf16[1536,512]{1,0:T(8,128)(2,1)}) %all-gather.9.cloned.1.call-update) | async-done | bytes 1572880 | tf_op jit(solution)/shard_map/all_gather | solution.py:110
  148.5 1.8 fusion.35
  150.4 27.6 %all_gather.35 = bf16[1024,128]{0,1:T(8,128)(2,1)S(1)} all-gather(bf16[128,128]{0,1:T(8,128)(2,1)S(1)} %slice.71), channel_id=1, replica_groups=mesh['grp'=2,'seq'=8,'col'=2] {'seq'}, dimensions={0}, use_global_device_ids=true | all-gather | bytes 294912 | tf_op jit(solution)/shard_map/all_gather | solution.py:124
  177.9 29.5 %all_gather.36 = bf16[1024,192]{0,1:T(8,128)(2,1)S(1)} all-gather(bf16[128,192]{0,1:T(8,128)(2,1)S(1)} %slice.72), channel_id=1, replica_groups=mesh['grp'=2,'seq'=8,'col'=2] {'seq'}, dimensions={0}, use_global_device_ids=true | all-gather | bytes 442368 | tf_op jit(solution)/shard_map/all_gather | solution.py:125
  209.6 3.3 %convolution_convert_fusion = bf16[128,1536]{1,0:T(8,128)(2,1)} fusion(bf16[128,768]{1,0:T(8,128)(2,1)S(1)} %reshape.52, bf16[768,1536]{0,1:T(8,128)(2,1)} %all-gather.11.cloned.1.call-done), kind=kOutput, calls=%fused_computation.10 | convolution fusion | flops 302186496 | bytes 2949120 | tf_op jit(solution)/shard_map/dot_general | solution.py:133
  212.9 5.2 %reduce-scatter.5.cloned.1.call-done = bf16[64,1536]{1,0:T(8,128)(2,1)} async-done(((bf16[128,1536]{1,0:T(8,128)(2,1)}), bf16[64,1536]{1,0:T(8,128)(2,1)}) %reduce-scatter.5.cloned.1.call-update) | async-done | bytes 196624 | tf_op jit(solution)/shard_map/reduce_scatter | solution.py:138
  218.1 1.7 convert_reduce_fusion
  220.0 1.8 all-gather.1
  221.9 26.4 %all_gather.39 = bf16[64,128]{1,0:T(8,128)(2,1)S(1)} all-gather(bf16[8,128]{1,0:T(8,128)(2,1)S(1)} %get-tuple-element.7), channel_id=1, replica_groups=mesh['grp'=2,'seq'=8,'col'=2] {'seq'}, dimensions={0}, use_global_device_ids=true | all-gather | bytes 18432 | tf_op jit(solution)/shard_map/all_gather | solution.py:150
  (60 shorter events, 8.8 us)
Async XLA Ops:
  7.2 212.6 %copy-start = (bf16[1536,256]{1,0:T(8,128)(2,1)S(1)}, bf16[1536,256]{1,0:T(8,128)(2,1)}, u32[]{:S(2)}) copy-start(bf16[1536,256]{1,0:T(8,128)(2,1)} %param.18) | copy-start | bytes 2359300
  7.2 24.2 %all-gather.13.cloned.1.call-start = ((), (), s32[]{:S(2)}) async-start(), calls=%async_computation.7 | async-start | bytes 2396160 | tf_op jit(solution)/shard_map/all_gather | solution.py:78
  8.7 6.2 %collective-permute-start = (bf16[2,704]{1,0:T(2,128)(2,1)S(1)}, bf16[2,704]{1,0:T(2,128)(2,1)S(1)}, u32[]{:S(2)}, u32[]{:S(2)}) collective-permute-start(bf16[2,704]{1,0:T(2,128)(2,1)S(1)} %get-tuple-element.4), channel_id=1, source_target_pairs={{0,2},{2,4},{4,6},{6,8},{8,10},{10,12},{12,14},{1,3},{3,5},{5,7},{... | collective-permute-start | bytes 8456 | tf_op jit(solution)/shard_map/ppermute | solution.py:19
  13.6 5.5 %collective-permute-start.1 = (bf16[2,704]{1,0:T(2,128)(2,1)S(1)}, bf16[2,704]{1,0:T(2,128)(2,1)S(1)}, u32[]{:S(2)}, u32[]{:S(2)}) collective-permute-start(bf16[2,704]{1,0:T(2,128)(2,1)S(1)} %get-tuple-element.5), channel_id=1, source_target_pairs={{2,0},{4,2},{6,4},{8,6},{10,8},{12,10},{14,12},{3,1},{5,3},{7,5},{... | collective-permute-start | bytes 8456 | tf_op jit(solution)/shard_map/ppermute | solution.py:20
  20.2 66.3 %all-gather.7.cloned.1.call-start = ((), (), s32[]{:S(2)}) async-start(), calls=%async_computation.2 | async-start | bytes 2654208 | tf_op jit(solution)/shard_map/all_gather | solution.py:90
  21.0 105.3 %reduce-scatter.3.cloned.1.call-start = ((), (), s32[]{:S(2)}) async-start(), calls=%async_computation.3 | async-start | bytes 589824 | tf_op jit(solution)/shard_map/reduce_scatter | solution.py:92
  41.0 2.9 %copy-start.1 = (f32[1408,516]{0,1:T(8,128)S(1)}, f32[1408,516]{0,1:T(8,128)}, u32[]{:S(2)}) copy-start(f32[1408,516]{0,1:T(8,128)} %reshape.62) | copy-start | bytes 8718340
  41.0 2.9 %copy-start.9 = (f32[1408]{0:T(1024)S(1)}, f32[1408]{0:T(1024)}, u32[]{:S(2)}) copy-start(f32[1408]{0:T(1024)} %param.12) | copy-start | bytes 16900
  45.1 4.4 %copy-start.4 = (bf16[5,1408,704]{1,2,0:T(8,128)(2,1)S(1)}, bf16[5,1408,704]{1,2,0:T(8,128)(2,1)}, u32[]{:S(2)}) copy-start(bf16[5,1408,704]{1,2,0:T(8,128)(2,1)} %param.11) | copy-start | bytes 29736964
  52.2 1.4 copy-start.2
  59.4 30.5 %copy-start.7 = (bf16[192,1024]{1,0:T(8,128)(2,1)S(1)}, bf16[192,1024]{1,0:T(8,128)(2,1)}, u32[]{:S(2)}) copy-start(bf16[192,1024]{1,0:T(8,128)(2,1)} %param.15) | copy-start | bytes 1179652
  59.4 31.3 %copy-start.5 = (bf16[1536,192]{0,1:T(8,128)(2,1)S(1)}, bf16[1536,192]{0,1:T(8,128)(2,1)}, u32[]{:S(2)}) copy-start(bf16[1536,192]{0,1:T(8,128)(2,1)} %param.17) | copy-start | bytes 1769476
  59.4 32.1 %copy-start.6 = (bf16[192,320]{1,0:T(8,128)(2,1)S(1)}, bf16[192,320]{1,0:T(8,128)(2,1)}, u32[]{:S(2)}) copy-start(bf16[192,320]{1,0:T(8,128)(2,1)} %param.16) | copy-start | bytes 368644
  89.9 37.5 %copy-start.10 = (f32[1536]{0:T(1024)S(1)}, f32[1536]{0:T(1024)}, u32[]{:S(2)}) copy-start(f32[1536]{0:T(1024)} %param.14) | copy-start | bytes 18436
  89.9 58.6 %all-gather.9.cloned.1.call-start = ((), (), s32[]{:S(2)}) async-start(), calls=%async_computation.4 | async-start | bytes 1769472 | tf_op jit(solution)/shard_map/all_gather | solution.py:110
  90.7 118.9 %all-gather.11.cloned.1.call-start = ((), (), s32[]{:S(2)}) async-start(), calls=%async_computation.5 | async-start | bytes 2654208 | tf_op jit(solution)/shard_map/all_gather | solution.py:135
  91.5 126.6 %reduce-scatter.5.cloned.1.call-start = ((), (), s32[]{:S(2)}) async-start(), calls=%async_computation.6 | async-start | bytes 589824 | tf_op jit(solution)/shard_map/reduce_scatter | solution.py:138
  209.2 8.9 %copy-start.3 = (bf16[64,1536]{1,0:T(8,128)(2,1)S(1)}, bf16[64,1536]{1,0:T(8,128)(2,1)}, u32[]{:S(2)}) copy-start(bf16[64,1536]{1,0:T(8,128)(2,1)} %reduce-scatter.3.cloned.1.call-done) | copy-start | bytes 589828
  209.5 38.8 %copy-start.8 = (bf16[128,128]{1,0:T(8,128)(2,1)S(1)}, bf16[128,128]{1,0:T(8,128)(2,1)}, u32[]{:S(2)}) copy-start(bf16[128,128]{1,0:T(8,128)(2,1)} %param.19) | copy-start | bytes 98308
Sparse Core Ops, SparseCore 0:
  20.3 10.9 all-gather.12
  33.5 52.9 all-gather.6
  90.0 6.3 reduce-scatter.2
  99.0 49.4 all-gather.8
  150.5 55.1 all-gather.10
  213.0 5.0 reduce-scatter.4
where the time goes:
time: 257 us; the launch traced here: 256 us
  blocking collectives  122 us (47%)
  waiting for transfers between devices  64.9 us (25%)
  matrix products  19.5 us (8%)
  local copies, waits for them, and re-layouts  18.4 us (7%)
  between operations  14.4 us (6%)
  other arithmetic  10.1 us (4%)
  starting transfers between devices  6.43 us (3%)
    all_gather x1, blocking collectives, on_device(): lax.all_gather(keyvalue_weight, 'seq', axis=0, tiled=True)  34.7 us
    all_gather x1, blocking collectives, on_device(): lax.all_gather(keyvalue[:, DK:], 'seq', axis=0, tiled=True)  29.5 us
    all_gather x1, blocking collectives, on_device(): lax.all_gather(keyvalue[:, :DK], 'seq', axis=0, tiled=True)  27.6 us
    all_gather x1, waiting for transfers between devices, on_device(): embed_full = lax.all_gather(embed_weight, 'seq', axis=1, tiled=True)  27.1 us
    all_gather x1, blocking collectives, on_device(): lax.all_gather(row_block[:, features:], 'seq', axis=0, tiled=True)  26.4 us
    all_gather x1, waiting for transfers between devices, on_device(): lax.all_gather(query_half, 'seq', axis=0, tiled=True)  17.2 us
    all_gather x1, waiting for transfers between devices, on_device(): widened = lax.all_gather(padded, 'col', axis=1, tiled=True)  10.3 us
    convert_element_type x2, local copies, waits for them, and re-layouts, on_device(): widened.astype(jnp.float32)  9.6 us
  transfers between devices with their start and end apart: 8, of which 5 were waited for; matrix products, arithmetic and copies ran while one was open for 13% of the time, Pallas kernels for 0%

commit v1 on v0

--- a/solution.py
+++ b/solution.py
@@ -7,6 +7,28 @@
 DV = 192
 POOL = 4
 PAIR_POOL = 16
+
+
+def joined_along(blocks, dim):
+    shape = list(blocks.shape[1:])
+    shape[dim] *= blocks.shape[0]
+    return jnp.moveaxis(blocks, 0, dim).reshape(shape)
+
+
+def doubled(array, axis):
+    size = lax.axis_size(axis)
+    blocks = array[None]
+    for level in range(size.bit_length() - 1):
+        bit = 1 << level
+        other = lax.ppermute(blocks, axis, [(i, i ^ bit) for i in range(size)])
+        both = jnp.stack([blocks, other])
+        upper = lax.axis_index(axis) >> level & 1
+        blocks = jnp.where(upper == 0, both, both[::-1]).reshape(-1, *array.shape)
+    return blocks
+
+
+def collect(x, axis, dim):
+    return joined_along(doubled(x, axis), dim)
 
 
 def with_halo(array, sides, width):
@@ -106,9 +128,7 @@
         query_weight, col_index * local_heads * DK, local_heads * DK, 1
     )
     query_sum = jnp.dot(
-        group_tokens,
-        lax.all_gather(query_half, "seq", axis=0, tiled=True),
-        preferred_element_type=jnp.float32,
+        group_tokens, collect(query_half, "seq", 0), preferred_element_type=jnp.float32
     )
     keyvalue_sum = jnp.dot(
         group_tokens,

time: 257 us -> 283 us (1.10)
  blocking collectives: 122 us -> 157 us
  waiting for transfers between devices: 64.9 us -> 52.2 us
  starting transfers between devices: 6.43 us -> 13.1 us
    all_gather x1, blocking collectives: 34.7 us -> 72.1 us  [on_device(): lax.all_gather(keyvalue_weight, 'seq', axis=0, tiled=True)]
    all_gather x1 -> x0, waiting for transfers between devices: 17.2 us -> none  [on_device(): lax.all_gather(query_half, 'seq', axis=0, tiled=True)]
    ppermute x0 -> x3, waiting for transfers between devices: none -> 7.17 us  [doubled(): other = lax.ppermute(blocks, axis, [(i, i ^ bit) for i in range(size)])]
    ppermute x0 -> x3, starting transfers between devices: none -> 6.61 us  [doubled(): other = lax.ppermute(blocks, axis, [(i, i ^ bit) for i in range(size)])]
  transfers between devices with their start and end apart: 8 -> 10, of which waited for: 5 -> 5; matrix products, arithmetic and copies ran while one was open for 13% -> 13% of each run, Pallas kernels for 0% -> 0%
where the time goes in v1:
time: 283 us
  blocking collectives  157 us (55%)
  waiting for transfers between devices  52.2 us (18%)
  matrix products  18.2 us (6%)
  local copies, waits for them, and re-layouts  17.7 us (6%)
  between operations  14.1 us (5%)
  starting transfers between devices  13.1 us (5%)
  other arithmetic  10.9 us (4%)
    all_gather x1, blocking collectives, on_device(): lax.all_gather(keyvalue_weight, 'seq', axis=0, tiled=True)  72.1 us
    all_gather x1, blocking collectives, on_device(): lax.all_gather(keyvalue[:, DK:], 'seq', axis=0, tiled=True)  27.3 us
    all_gather x1, waiting for transfers between devices, on_device(): embed_full = lax.all_gather(embed_weight, 'seq', axis=1, tiled=True)  27.1 us
    all_gather x1, blocking collectives, on_device(): lax.all_gather(keyvalue[:, :DK], 'seq', axis=0, tiled=True)  26.8 us
    all_gather x1, blocking collectives, on_device(): lax.all_gather(row_block[:, features:], 'seq', axis=0, tiled=True)  26.4 us
    convert_element_type x2, local copies, waits for them, and re-layouts, on_device(): widened.astype(jnp.float32)  9.61 us
    dot_general x5, matrix products, on_device(): jnp.dot(activated[tap_index:tap_index + positions], conv_weight[tap_index...  8.49 us
    all_gather x1, waiting for transfers between devices, on_device(): widened = lax.all_gather(padded, 'col', axis=1, tiled=True)  7.79 us
  transfers between devices with their start and end apart: 10, of which 5 were waited for; matrix products, arithmetic and copies ran while one was open for 13% of the time, Pallas kernels for 0%

profile of v1, /device:TPU:0, one launch (start us, length us, event | category | flops | bytes accessed | tf_op | source)
XLA Modules:
  0.0 282.8 jit_solution(16774767881286605527)
XLA Ops:
  7.2 1.4 copy.19
  8.7 5.0 %collective-permute-start = (bf16[2,704]{1,0:T(2,128)(2,1)S(1)}, bf16[2,704]{1,0:T(2,128)(2,1)S(1)}, u32[]{:S(2)}, u32[]{:S(2)}) collective-permute-start(bf16[2,704]{1,0:T(2,128)(2,1)S(1)} %get-tuple-element.4), channel_id=1, source_target_pairs={{0,2},{2,4},{4,6},{6,8},{8,10},{10,12},{12,14},{1,3},{3,5},{5,7},{... | collective-permute-start | bytes 8456 | tf_op jit(solution)/shard_map/ppermute | solution.py:41
  13.7 1.3 collective-permute-start.1
  15.1 4.2 %collective-permute-done.1 = bf16[2,704]{1,0:T(2,128)(2,1)S(1)} collective-permute-done((bf16[2,704]{1,0:T(2,128)(2,1)S(1)}, bf16[2,704]{1,0:T(2,128)(2,1)S(1)}, u32[]{:S(2)}, u32[]{:S(2)}) %collective-permute-start.1) | collective-permute-done | bytes 2848 | tf_op jit(solution)/shard_map/ppermute | solution.py:42
  21.2 2.5 collective-permute-start.2
  23.7 7.8 %all-gather.10.cloned.1.call-done = bf16[2,704,516]{1,2,0:T(8,128)(2,1)} async-done(((bf16[1,704,516]{1,2,0:T(8,128)(2,1)}), bf16[2,704,516]{1,2,0:T(8,128)(2,1)}) %all-gather.10.cloned.1.call-update) | async-done | bytes 1453072 | tf_op jit(solution)/shard_map/all_gather | solution.py:100
  31.5 4.3 %copy.22 = f32[2,704,516]{1,0,2:T(2,128)} copy(bf16[2,704,516]{1,2,0:T(8,128)(2,1)} %all-gather.10.cloned.1.call-done) | data formatting | bytes 4359168 | tf_op jit(solution)/shard_map/convert_element_type | solution.py:102
  35.8 5.3 %reshape.70 = f32[1408,516]{0,1:T(8,128)} reshape(f32[2,704,516]{1,0,2:T(2,128)} %copy.22) | data formatting | bytes 5812224 | tf_op jit(solution)/shard_map/convert_element_type | solution.py:102
  41.1 2.4 multiply_reduce_fusion
  44.0 1.2 fusion.7
  45.3 3.0 %fusion.16 = f32[512,704]{0,1:T(8,128)S(1)} fusion(bf16[5,1408,704]{1,2,0:T(8,128)(2,1)} %param.11, bf16[516,1408]{1,0:T(8,128)(2,1)S(1)} %fusion.7), kind=kOutput, calls=%fused_computation.22 | convolution fusion | flops 1015021568 | bytes 4866048 | tf_op jit(solution)/shard_map/dot_general | solution.py:106
  48.3 1.4 copy-done.4
  49.7 1.3 fusion.12
  51.0 1.3 fusion.10
  52.4 1.3 fusion.8
  53.7 1.5 add_add_fusion
  55.2 1.6 copy.23
  56.9 1.8 reshape.56
  59.6 27.1 %all-gather.6.cloned.1.call-done = bf16[704,1536]{0,1:T(8,128)(2,1)} async-done(((bf16[704,192]{0,1:T(8,128)(2,1)}), bf16[704,1536]{0,1:T(8,128)(2,1)}) %all-gather.6.cloned.1.call-update) | async-done | bytes 2162704 | tf_op jit(solution)/shard_map/all_gather | solution.py:112
  86.7 3.3 %convolution_convert_fusion.1 = bf16[128,1536]{1,0:T(8,128)(2,1)} fusion(bf16[704,1536]{0,1:T(8,128)(2,1)} %all-gather.6.cloned.1.call-done, f32[128,704]{1,0:T(8,128)S(1)} %reduce_sum.46), kind=kOutput, calls=%fused_computation.11 | convolution fusion | flops 277200896 | bytes 2916352 | tf_op jit(solution)/shard_map/dot_general | solution.py:115
  90.2 1.6 collective-permute-start.3
  92.6 7.2 %collective-permute-done.3 = bf16[2,192,512]{2,1,0:T(8,128)(2,1)S(1)} collective-permute-done((bf16[2,192,512]{2,1,0:T(8,128)(2,1)S(1)}, bf16[2,192,512]{2,1,0:T(8,128)(2,1)S(1)}, u32[]{:S(2)}, u32[]{:S(2)}) %collective-permute-start.3) | collective-permute-done | bytes 393248 | tf_op jit(solution)/shard_map/ppermute | solution.py:23
  100.0 2.6 collective-permute-start.4
  102.6 72.1 %all_gather.30 = bf16[1536,320]{1,0:T(8,128)(2,1)S(1)} all-gather(bf16[192,320]{1,0:T(8,128)(2,1)} %param.16), channel_id=1, replica_groups=mesh['grp'=2,'seq'=8,'col'=2] {'seq'}, dimensions={0}, use_global_device_ids=true | all-gather | bytes 1105920 | tf_op jit(solution)/shard_map/all_gather | solution.py:135
  177.4 2.1 all_gather.29
  180.5 26.8 %all_gather.31 = bf16[1024,128]{0,1:T(8,128)(2,1)S(1)} all-gather(bf16[128,128]{0,1:T(8,128)(2,1)S(1)} %slice.71), channel_id=1, replica_groups=mesh['grp'=2,'seq'=8,'col'=2] {'seq'}, dimensions={0}, use_global_device_ids=true | all-gather | bytes 294912 | tf_op jit(solution)/shard_map/all_gather | solution.py:144
  207.4 27.3 %all_gather.32 = bf16[1024,192]{0,1:T(8,128)(2,1)S(1)} all-gather(bf16[128,192]{0,1:T(8,128)(2,1)S(1)} %slice.72), channel_id=1, replica_groups=mesh['grp'=2,'seq'=8,'col'=2] {'seq'}, dimensions={0}, use_global_device_ids=true | all-gather | bytes 442368 | tf_op jit(solution)/shard_map/all_gather | solution.py:145
  236.7 3.4 %convolution_convert_fusion = bf16[128,1536]{1,0:T(8,128)(2,1)} fusion(bf16[128,768]{1,0:T(8,128)(2,1)S(1)} %reshape.60, bf16[768,1536]{0,1:T(8,128)(2,1)} %all-gather.8.cloned.1.call-done), kind=kOutput, calls=%fused_computation.10 | convolution fusion | flops 302186496 | bytes 2949120 | tf_op jit(solution)/shard_map/dot_general | solution.py:153
  240.1 5.1 %reduce-scatter.5.cloned.1.call-done = bf16[64,1536]{1,0:T(8,128)(2,1)} async-done(((bf16[128,1536]{1,0:T(8,128)(2,1)}), bf16[64,1536]{1,0:T(8,128)(2,1)}) %reduce-scatter.5.cloned.1.call-update) | async-done | bytes 196624 | tf_op jit(solution)/shard_map/reduce_scatter | solution.py:158
  245.2 1.7 convert_reduce_fusion
  247.1 1.8 all-gather.1
  249.0 26.4 %all_gather.35 = bf16[64,128]{1,0:T(8,128)(2,1)S(1)} all-gather(bf16[8,128]{1,0:T(8,128)(2,1)S(1)} %get-tuple-element.11), channel_id=1, replica_groups=mesh['grp'=2,'seq'=8,'col'=2] {'seq'}, dimensions={0}, use_global_device_ids=true | all-gather | bytes 18432 | tf_op jit(solution)/shard_map/all_gather | solution.py:170
  (67 shorter events, 11.5 us)
Async XLA Ops:
  7.2 239.7 %copy-start = (bf16[1536,256]{1,0:T(8,128)(2,1)S(1)}, bf16[1536,256]{1,0:T(8,128)(2,1)}, u32[]{:S(2)}) copy-start(bf16[1536,256]{1,0:T(8,128)(2,1)} %param.18) | copy-start | bytes 2359300
  7.2 24.3 %all-gather.10.cloned.1.call-start = ((), (), s32[]{:S(2)}) async-start(), calls=%async_computation.6 | async-start | bytes 2396160 | tf_op jit(solution)/shard_map/all_gather | solution.py:100
  8.7 12.5 %copy-start.6 = (bf16[192,1024]{1,0:T(8,128)(2,1)S(1)}, bf16[192,1024]{1,0:T(8,128)(2,1)}, u32[]{:S(2)}) copy-start(bf16[192,1024]{1,0:T(8,128)(2,1)} %param.15) | copy-start | bytes 1179652
  8.7 6.3 %collective-permute-start = (bf16[2,704]{1,0:T(2,128)(2,1)S(1)}, bf16[2,704]{1,0:T(2,128)(2,1)S(1)}, u32[]{:S(2)}, u32[]{:S(2)}) collective-permute-start(bf16[2,704]{1,0:T(2,128)(2,1)S(1)} %get-tuple-element.4), channel_id=1, source_target_pairs={{0,2},{2,4},{4,6},{6,8},{8,10},{10,12},{12,14},{1,3},{3,5},{5,7},{... | collective-permute-start | bytes 8456 | tf_op jit(solution)/shard_map/ppermute | solution.py:41
  13.7 5.5 %collective-permute-start.1 = (bf16[2,704]{1,0:T(2,128)(2,1)S(1)}, bf16[2,704]{1,0:T(2,128)(2,1)S(1)}, u32[]{:S(2)}, u32[]{:S(2)}) collective-permute-start(bf16[2,704]{1,0:T(2,128)(2,1)S(1)} %get-tuple-element.5), channel_id=1, source_target_pairs={{2,0},{4,2},{6,4},{8,6},{10,8},{12,10},{14,12},{3,1},{5,3},{7,5},{... | collective-permute-start | bytes 8456 | tf_op jit(solution)/shard_map/ppermute | solution.py:42
  20.4 66.3 %all-gather.6.cloned.1.call-start = ((), (), s32[]{:S(2)}) async-start(), calls=%async_computation.2 | async-start | bytes 2654208 | tf_op jit(solution)/shard_map/all_gather | solution.py:112
  21.1 154.1 %reduce-scatter.3.cloned.1.call-start = ((), (), s32[]{:S(2)}) async-start(), calls=%async_computation.3 | async-start | bytes 589824 | tf_op jit(solution)/shard_map/reduce_scatter | solution.py:114
  21.2 68.9 %collective-permute-start.2 = (bf16[1,192,512]{2,1,0:T(8,128)(2,1)S(1)}, bf16[1,192,512]{2,1,0:T(8,128)(2,1)S(1)}, u32[]{:S(2)}, u32[]{:S(2)}) collective-permute-start(bf16[1,192,512]{2,1,0:T(8,128)(2,1)S(1)} %get-tuple-element.9), channel_id=1, source_target_pairs={{0,2},{2,0},{4,6},{6,4},{8,10},{10,8},{12,14},{14,12},{1,3},{3,1},... | collective-permute-start | bytes 589832 | tf_op jit(solution)/shard_map/ppermute | solution.py:23
  41.1 2.9 %copy-start.1 = (f32[1408,516]{0,1:T(8,128)S(1)}, f32[1408,516]{0,1:T(8,128)}, u32[]{:S(2)}) copy-start(f32[1408,516]{0,1:T(8,128)} %reshape.70) | copy-start | bytes 8718340
  41.1 2.9 %copy-start.8 = (f32[1408]{0:T(1024)S(1)}, f32[1408]{0:T(1024)}, u32[]{:S(2)}) copy-start(f32[1408]{0:T(1024)} %param.12) | copy-start | bytes 16900
  45.3 4.4 %copy-start.4 = (bf16[5,1408,704]{1,2,0:T(8,128)(2,1)S(1)}, bf16[5,1408,704]{1,2,0:T(8,128)(2,1)}, u32[]{:S(2)}) copy-start(bf16[5,1408,704]{1,2,0:T(8,128)(2,1)} %param.11) | copy-start | bytes 29736964
  52.4 1.4 copy-start.2
  90.0 1.8 copy-start.5
  90.0 146.7 %all-gather.8.cloned.1.call-start = ((), (), s32[]{:S(2)}) async-start(), calls=%async_computation.4 | async-start | bytes 2654208 | tf_op jit(solution)/shard_map/all_gather | solution.py:155
  90.2 9.5 %collective-permute-start.3 = (bf16[2,192,512]{2,1,0:T(8,128)(2,1)S(1)}, bf16[2,192,512]{2,1,0:T(8,128)(2,1)S(1)}, u32[]{:S(2)}, u32[]{:S(2)}) collective-permute-start(bf16[2,192,512]{2,1,0:T(8,128)(2,1)S(1)} %get-tuple-element.7), channel_id=1, source_target_pairs={{0,4},{2,6},{4,0},{6,2},{8,12},{10,14},{12,8},{14,10},{1,5},{3,7},... | collective-permute-start | bytes 1179656 | tf_op jit(solution)/shard_map/ppermute | solution.py:23
  92.6 152.7 %reduce-scatter.5.cloned.1.call-start = ((), (), s32[]{:S(2)}) async-start(), calls=%async_computation.5 | async-start | bytes 589824 | tf_op jit(solution)/shard_map/reduce_scatter | solution.py:158
  100.0 74.7 %collective-permute-start.4 = (bf16[4,192,512]{2,1,0:T(8,128)(2,1)S(1)}, bf16[4,192,512]{2,1,0:T(8,128)(2,1)S(1)}, u32[]{:S(2)}, u32[]{:S(2)}) collective-permute-start(bf16[4,192,512]{2,1,0:T(8,128)(2,1)S(1)} %bitcast.61), channel_id=1, source_target_pairs={{0,8},{2,10},{4,12},{6,14},{8,0},{10,2},{12,4},{14,6},{1,9},{3,11}... | collective-permute-start | bytes 2359304 | tf_op jit(solution)/shard_map/ppermute | solution.py:23
  174.9 1.5 copy-start.9
  236.7 8.5 %copy-start.3 = (bf16[64,1536]{1,0:T(8,128)(2,1)S(1)}, bf16[64,1536]{1,0:T(8,128)(2,1)}, u32[]{:S(2)}) copy-start(bf16[64,1536]{1,0:T(8,128)(2,1)} %reduce-scatter.3.cloned.1.call-done) | copy-start | bytes 589828
  240.1 35.3 %copy-start.7 = (bf16[128,128]{1,0:T(8,128)(2,1)S(1)}, bf16[128,128]{1,0:T(8,128)(2,1)}, u32[]{:S(2)}) copy-start(bf16[128,128]{1,0:T(8,128)(2,1)} %param.19) | copy-start | bytes 98308
Sparse Core Ops, SparseCore 0:
  20.5 10.9 all-gather.9
  33.7 52.9 all-gather.5
  90.2 6.3 reduce-scatter.2
  98.6 84.9 all-gather.7
  240.2 4.9 reduce-scatter.4
